TPU v7x, 256 devices: a whole 4x4x8 slice. The times are simulated.
256 devices in a mesh: dp: 8 (over z_hi, x), expert: 32 (over z_lo, y, core).
Axes of the slice: x: 4, y: 4, z: 8 (z_hi: 2, z_lo: 4; z = z_hi * 4 + z_lo), core: 2. Of those that a mesh axis runs over, the one named last changes fastest.
Arguments:
- tokens: bfloat16 [32768, 3584], P(('dp', 'expert')), may hold values from -6 to 6
- cotangent: bfloat16 [32768, 3584], P(('dp', 'expert')), may hold values from -0.09375 to 0.09375
- expert_ids: int32 [32768, 8], P(('dp', 'expert')), may hold values from 0 to 255, all different within a row; in each aligned block of 128 rows (0 to 127, 128 to 255, ...) at most 6 rows name the same one
- gates: bfloat16 [32768, 8], P(('dp', 'expert')), may hold values from 0.049804688 to 1
- swap_flags: int32 [16], replicated, may hold values 0 or 1
- gate_w: bfloat16 [32, 3584, 1024], P('expert', None, 'dp'), may hold values from -0.09375 to 0.09375
- up_w: bfloat16 [32, 3584, 1024], P('expert', None, 'dp'), may hold values from -0.09375 to 0.09375
- down_w: bfloat16 [32, 1024, 3584], P('expert', 'dp'), may hold values from -0.1875 to 0.1875
Outputs:
- grad_gate_w: bfloat16 [32, 3584, 1024], P('expert', None, 'dp')
- grad_up_w: bfloat16 [32, 3584, 1024], P('expert', None, 'dp')
- grad_down_w: bfloat16 [32, 1024, 3584], P('expert', 'dp')
- score_grad: float32 [32768, 8], P(('dp', 'expert'))
Inputs may be any that keep to these rules, and one draw needn't show every extreme that they name: `expert_ids`: among the 128 rows of one device no expert is named more than 6 times, a bound that some block reaches; the numbers of one row differ. `swap_flags`: 1 means that slots s and s + 16 trade their experts.
All inputs are finite; a program needn't handle non-finite values.
Results may differ from a plain program's by a relative error of at most 0.011.
Values may be sent and summed in bfloat16 or wider, within the bound.
A program may use at most 128 MiB of HBM per device.

v0:
```python
import functools

import jax
import jax.numpy as jnp
from jax import lax
from jax.experimental import pallas as pl
from jax.experimental.pallas import tpu as pltpu
from jax.sharding import PartitionSpec as P

CAP = 6
LANE = 128


def partner(block, axis, stride):
    count = lax.axis_size(axis)
    route = []
    for low in range(count):
        high = low | 1 << stride
        if high != low and high < count:
            route += [(low, high), (high, low)]
    return lax.ppermute(block, axis, route)


def dp_gather_kernel(n_dp, ring, chunks, x_ref, o_ref, recv, recv_z, send):
    me = lax.axis_index("dp")
    ex = lax.axis_index("expert")
    rows = x_ref.shape[1]
    half = rows // 2
    piece = rows // chunks
    plane = me // ring
    pos = me % ring
    left = plane * ring + (pos + ring - 1) % ring
    right = plane * ring + (pos + 1) % ring
    far = plane * ring + (pos + 2) % ring
    across = (me + ring) % n_dp

    def span(k, start, size):
        return o_ref.at[:, pl.ds(k * rows + start, size), :]

    def push(src, dst, slot, sem, peer):
        copy = pltpu.make_async_remote_copy(
            src_ref=src,
            dst_ref=dst,
            send_sem=send.at[slot],
            recv_sem=sem,
            device_id=(peer, ex),
            device_id_type=pl.DeviceIdType.MESH,
        )
        copy.start()
        return copy

    def arrived(ref, sem):
        pltpu.make_async_copy(ref, ref, sem).wait()

    barrier = pltpu.get_barrier_semaphore()
    for peer in (left, right, across):
        pl.semaphore_signal(barrier, inc=1, device_id=(peer, ex), device_id_type=pl.DeviceIdType.MESH)
    pl.semaphore_wait(barrier, 3)

    sent = []
    for q in range(chunks):
        sent.append(
            push(
                x_ref.at[:, pl.ds(q * piece, piece), :],
                span(me, q * piece, piece),
                len(sent),
                recv_z.at[q],
                across,
            )
        )
    sent.append(push(x_ref, span(me, 0, rows), len(sent), recv.at[me], left))
    sent.append(push(x_ref, span(me, 0, rows), len(sent), recv.at[me], right))
    arrived(span(left, 0, rows), recv.at[left])
    sent.append(push(span(left, 0, half), span(left, 0, half), len(sent), recv.at[left], right))
    arrived(span(right, 0, rows), recv.at[right])
    sent.append(push(span(right, half, half), span(right, half, half), len(sent), recv.at[right], left))
    for q in range(chunks):
        chunk = span(across, q * piece, piece)
        arrived(chunk, recv_z.at[q])
        sent.append(push(chunk, chunk, len(sent), recv.at[across], left))
        sent.append(push(chunk, chunk, len(sent), recv.at[across], right))
    left_across = (left + ring) % n_dp
    right_across = (right + ring) % n_dp
    arrived(span(left_across, 0, rows), recv.at[left_across])
    sent.append(
        push(span(left_across, 0, half), span(left_across, 0, half), len(sent), recv.at[left_across], right)
    )
    arrived(span(right_across, 0, rows), recv.at[right_across])
    sent.append(
        push(span(right_across, half, half), span(right_across, half, half), len(sent), recv.at[right_across], left)
    )
    local = pltpu.make_async_copy(x_ref, span(me, 0, rows), recv.at[me])
    local.start()
    arrived(span(far, 0, rows), recv.at[far])
    far_across = (far + ring) % n_dp
    arrived(span(far_across, 0, rows), recv.at[far_across])
    local.wait()
    for copy in sent:
        copy.wait_send()


def dp_gather(block):
    n_dp = lax.axis_size("dp")
    ring = n_dp // 2
    chunks = 4
    cap, rows, row_width = block.shape
    sends = 3 * chunks + 6
    return pl.pallas_call(
        functools.partial(dp_gather_kernel, n_dp, ring, chunks),
        out_shape=jax.ShapeDtypeStruct((cap, n_dp * rows, row_width), block.dtype),
        in_specs=[pl.BlockSpec(memory_space=pl.ANY)],
        out_specs=pl.BlockSpec(memory_space=pl.ANY),
        scratch_shapes=[
            pltpu.SemaphoreType.DMA((n_dp,)),
            pltpu.SemaphoreType.DMA((chunks,)),
            pltpu.SemaphoreType.DMA((sends,)),
        ],
        compiler_params=pltpu.CompilerParams(collective_id=0, has_side_effects=True),
    )(block)


def expert_exchange_kernel(n_ex, x_ref, o_ref, recv, send, local_sem):
    me = lax.axis_index("expert")
    dp = lax.axis_index("dp")
    barrier = pltpu.get_barrier_semaphore()
    for step in range(1, n_ex):
        peer = (me + step) % n_ex
        pl.semaphore_signal(barrier, inc=1, device_id=(dp, peer), device_id_type=pl.DeviceIdType.MESH)
    pl.semaphore_wait(barrier, n_ex - 1)
    local = pltpu.make_async_copy(x_ref.at[pl.ds(me, 1)], o_ref.at[pl.ds(me, 1)], local_sem.at[0])
    local.start()
    sent = []
    for step in range(1, n_ex):
        peer = (me + step) % n_ex
        copy = pltpu.make_async_remote_copy(
            src_ref=x_ref.at[pl.ds(peer, 1)],
            dst_ref=o_ref.at[pl.ds(me, 1)],
            send_sem=send.at[step],
            recv_sem=recv.at[0],
            device_id=(dp, peer),
            device_id_type=pl.DeviceIdType.MESH,
        )
        copy.start()
        sent.append(copy)
    pltpu.make_async_copy(
        x_ref.at[pl.ds(0, n_ex - 1)], o_ref.at[pl.ds(0, n_ex - 1)], recv.at[0]
    ).wait()
    local.wait()
    for copy in sent:
        copy.wait_send()


def expert_exchange(block):
    n_ex = lax.axis_size("expert")
    return pl.pallas_call(
        functools.partial(expert_exchange_kernel, n_ex),
        out_shape=jax.ShapeDtypeStruct(block.shape, block.dtype),
        in_specs=[pl.BlockSpec(memory_space=pl.ANY)],
        out_specs=pl.BlockSpec(memory_space=pl.ANY),
        scratch_shapes=[
            pltpu.SemaphoreType.DMA((1,)),
            pltpu.SemaphoreType.DMA((n_ex,)),
            pltpu.SemaphoreType.DMA((1,)),
        ],
        compiler_params=pltpu.CompilerParams(collective_id=1, has_side_effects=True),
    )(block)


def body(tokens, cotangent, expert_ids, gates, swap_flags, gate_w, up_w, down_w):
    axis_len = lax.axis_size("expert")
    half_axis = axis_len // 2
    pair_bit = axis_len.bit_length() - 2
    own_slot = lax.axis_index("expert")
    tok_count = tokens.shape[0]
    top_count = expert_ids.shape[1]
    width = tokens.shape[1]
    flat_ids = expert_ids.reshape(-1)
    choice_count = flat_ids.shape[0]
    valid = flat_ids < axis_len
    pair_index = jnp.arange(half_axis, dtype=jnp.int32)
    flag_of = jnp.sum(
        jnp.where((flat_ids % half_axis)[:, None] == pair_index[None, :], swap_flags[None, :], 0),
        axis=1,
    )
    own_flag = jnp.sum(jnp.where(pair_index == own_slot % half_axis, swap_flags, 0))
    target = jnp.where(flag_of == 1, jnp.bitwise_xor(flat_ids, half_axis), flat_ids)
    target = jnp.where(valid, target, 0)
    onehot = (
        (target[:, None] == jnp.arange(axis_len, dtype=jnp.int32)[None, :]) & valid[:, None]
    ).astype(jnp.bfloat16)
    order = jnp.arange(choice_count, dtype=jnp.int32)
    lower = (order[None, :] <= order[:, None]).astype(jnp.bfloat16)
    counts = jnp.dot(lower, onehot, preferred_element_type=jnp.float32)
    ranks = jnp.sum(counts * onehot.astype(jnp.float32), axis=1).astype(jnp.int32) - 1
    slot_count = axis_len * CAP
    slots = jnp.where(valid, target * CAP + ranks, slot_count)
    pick = (slots[:, None] == jnp.arange(slot_count, dtype=jnp.int32)[None, :]).astype(jnp.bfloat16)
    token_pick = jnp.sum(pick.reshape(tok_count, top_count, slot_count).astype(jnp.float32), axis=1)
    token_pick = token_pick.astype(jnp.bfloat16)
    rows_xdy = lax.dot_general(
        token_pick,
        jnp.concatenate([tokens, cotangent], axis=1),
        (((0,), (0,)), ((), ())),
        preferred_element_type=jnp.float32,
    ).astype(tokens.dtype)
    send_g = jnp.dot(gates.reshape(1, -1), pick, preferred_element_type=jnp.float32).astype(gates.dtype)
    g_cols = jnp.where(
        jnp.arange(LANE, dtype=jnp.int32)[None, :] == 0, send_g.reshape(-1, 1), jnp.zeros((), gates.dtype)
    )
    packed = jnp.concatenate([rows_xdy, g_cols], axis=1)
    row_width = packed.shape[1]
    packed = packed.reshape(axis_len, CAP * row_width // LANE, LANE)
    recv = expert_exchange(packed).reshape(axis_len, CAP, row_width)
    recv = jnp.transpose(recv, (1, 0, 2))
    recv, gate_w, up_w, down_w = lax.optimization_barrier((recv, gate_w, up_w, down_w))
    w_gate = gate_w[0]
    w_up = up_w[0]
    w_down = down_w[0]
    other_gate, other_up, other_down = partner((gate_w, up_w, down_w), "expert", pair_bit)
    taken = own_flag == 1
    w_gate = jnp.where(taken, other_gate[0], w_gate)
    w_up = jnp.where(taken, other_up[0], w_up)
    w_down = jnp.where(taken, other_down[0], w_down)
    gathered = dp_gather(recv)
    block_count = lax.axis_size("dp")
    row_x = gathered[:, :, :width]
    row_dy = gathered[:, :, width:2 * width]
    row_g = gathered[:, :, 2 * width:2 * width + 1]
    feature = (((2,), (0,)), ((), ()))
    rows_contract = (((0, 1), (0, 1)), ((), ()))
    hidden_count = w_gate.shape[1]
    w_both = jnp.concatenate([w_gate, w_up], axis=1)
    pre_both = lax.dot_general(row_x, w_both, feature, preferred_element_type=jnp.float32)
    pre_gate = pre_both[:, :, :hidden_count]
    pre_up = pre_both[:, :, hidden_count:]
    sigma = jax.nn.sigmoid(pre_gate)
    active = pre_gate * sigma
    hidden = (active * pre_up).astype(jnp.bfloat16)
    back = lax.dot_general(
        row_dy, w_down, (((2,), (1,)), ((), ())), preferred_element_type=jnp.float32
    )
    score = jnp.sum(hidden.astype(jnp.float32) * back, axis=2).T
    scaled = row_dy * row_g
    d_hidden = row_g.astype(jnp.float32) * back
    d_gate = (d_hidden * pre_up * sigma * (1.0 + pre_gate * (1.0 - sigma))).astype(jnp.bfloat16)
    d_up = (d_hidden * active).astype(jnp.bfloat16)
    d_both = jnp.concatenate([d_gate, d_up], axis=2)
    grad_both = lax.dot_general(row_x, d_both, rows_contract, preferred_element_type=jnp.float32)
    grad_gate = grad_both[:, :hidden_count]
    grad_up = grad_both[:, hidden_count:]
    grad_down = lax.dot_general(hidden, scaled, rows_contract, preferred_element_type=jnp.float32)
    scores = score.reshape(block_count, axis_len * CAP)
    parts = lax.all_to_all(scores, "dp", split_axis=0, concat_axis=0, tiled=True)
    own_scores = jnp.sum(parts, axis=0).reshape(axis_len, CAP)
    returned = lax.all_to_all(own_scores, "expert", split_axis=0, concat_axis=0, tiled=True)
    picked = jnp.sum(jnp.where(pick > 0, returned.reshape(1, -1), 0.0), axis=1)
    score_grad = jnp.where(valid, picked, 0.0).reshape(tok_count, top_count)
    out_gate = grad_gate.astype(jnp.bfloat16)[None]
    out_up = grad_up.astype(jnp.bfloat16)[None]
    out_down = grad_down.astype(jnp.bfloat16)[None]
    return (out_gate, out_up, out_down, score_grad)


def solution(mesh):
    placed = (
        P(("dp", "expert"), None),
        P(("dp", "expert"), None),
        P(("dp", "expert"), None),
        P(("dp", "expert"), None),
        P(),
        P("expert", None, "dp"),
        P("expert", None, "dp"),
        P("expert", "dp", None),
    )
    return jax.shard_map(
        body,
        mesh=mesh,
        in_specs=placed,
        out_specs=(
            P("expert", None, "dp"),
            P("expert", None, "dp"),
            P("expert", "dp", None),
            P(("dp", "expert"), None),
        ),
        check_vma=False,
    )
```

profile of v0, /device:TPU:1, one launch (start us, length us, event | category | flops | bytes accessed | tf_op | source)
XLA Modules:
  0.0 447.0 jit_solution(8170949506452680733)
XLA Ops:
  0.6 0.8 copy.53
  1.5 0.8 copy.48
  2.4 0.7 select_reduce_fusion.1
  4.5 2.3 convolution_convert_fusion
  7.0 4.5 %reshape.127.x_ref = bf16[32,342,128]{2,1,0:T(8,128)(2,1)} reshape(bf16[192,7296]{1,0:T(8,128)(2,1)S(1)} %pad_maximum_fusion) | data formatting | bytes 5603328 | tf_op jit(solution)/shard_map/reshape | solution.py:212
  11.5 60.9 %shard_map.111 = bf16[32,342,128]{2,1,0:T(8,128)(2,1)} custom-call(bf16[32,342,128]{2,1,0:T(8,128)(2,1)} %reshape.127.x_ref), custom_call_target="tpu_custom_call" | custom-call | tf_op jit(solution)/shard_map/pallas_call | solution.py:155
  72.5 6.3 %reshape.128 = bf16[32,6,7296]{2,1,0:T(8,128)(2,1)} reshape(bf16[32,342,128]{2,1,0:T(8,128)(2,1)} %shard_map.111) | data formatting | bytes 5603328 | tf_op jit(solution)/shard_map/reshape | solution.py:213
  78.8 4.0 copy.68
  83.3 16.0 %collective-permute-start.2 = (bf16[1,3584,128]{1,2,0:T(8,128)(2,1)S(1)}, bf16[1,3584,128]{1,2,0:T(8,128)(2,1)}, u32[]{:S(2)}, u32[]{:S(2)}) collective-permute-start(bf16[1,3584,128]{1,2,0:T(8,128)(2,1)S(1)} %copy.57), channel_id=1, source_target_pairs={{0,16},{16,0},{1,17},{17,1},{2,18},{18,2},{3,19},{19,3},{4,20},{20... | collective-permute-start | bytes 2752520 | tf_op jit(solution)/shard_map/ppermute | solution.py:21
  100.0 2.3 collective-permute-start
  102.3 284.9 %shard_map.112 = bf16[6,256,7296]{2,1,0:T(8,128)(2,1)} custom-call(bf16[6,32,7296]{2,1,0:T(8,128)(2,1)} %bitcast.40), custom_call_target="tpu_custom_call" | custom-call | tf_op jit(solution)/shard_map/pallas_call | solution.py:108
  387.3 1.2 slice_reduce_fusion
  390.2 8.5 %fusion.7 = f32[6,256,256]{1,2,0:T(8,128)} fusion(bf16[6,256,7296]{2,1,0:T(8,128)(2,1)} %shard_map.112, bf16[3584,128]{0,1:T(8,128)(2,1)S(1)} %select_bitcast_fusion, bf16[3584,128]{0,1:T(8,128)(2,1)S(1)} %select_bitcast_fusion.1), kind=kOutput, calls=%fused_computation.7 | convolution fusion | flops 2822242304 | bytes 14417920 | tf_op jit(solution)/shard_map/dot_general | solution.py:233
  398.6 0.9 slice-done.3
  399.6 1.2 slice-done.4
  401.3 5.2 %multiply_reduce_fusion = (f32[6,256]{1,0:T(8,128)S(1)}, bf16[6,256,128]{1,2,0:T(8,128)(2,1)S(1)}, bf16[6,256,128]{1,2,0:T(8,128)(2,1)S(1)}, bf16[6,256,128]{1,2,0:T(8,128)(2,1)S(1)}) fusion(f32[6,256,256]{1,2,0:T(8,128)} %fusion.7, f32[6,256]{1,0:T(8,128)S(1)} %mul.69, bf16[1,128,3584]{2,1,0:T(8,128)(2,1)} %collective-permute-done, ...), kind=kOutput, calls=%fused_computation.39 | convolution fusion | flops 1413478912 | bytes 15611905 | tf_op jit(solution)/shard_map/dot_general | solution.py:239
  406.7 0.7 all_to_all.16
  407.4 3.5 all-to-all-start
  411.0 7.2 %fusion.13 = bf16[3584,256]{1,0:T(8,128)(2,1)S(1)} fusion(bf16[6,256,7296]{2,1,0:T(8,128)(2,1)} %shard_map.112, bf16[6,256,128]{1,2,0:T(8,128)(2,1)S(1)} %get-tuple-element.31, bf16[6,256,128]{1,2,0:T(8,128)(2,1)S(1)} %get-tuple-element.32), kind=kOutput, calls=%fused_computation.12 | convolution fusion | flops 2821062656 | bytes 13631488 | tf_op jit(solution)/shard_map/dot_general | solution.py:248
  418.1 1.3 slice_bitcast_fusion
  419.7 0.7 all_to_all.14
  420.4 17.0 %all-to-all-start.1 = ((f32[32,1,6]{2,1,0:T(1,128)}), f32[32,1,6]{2,1,0:T(1,128)S(1)}, u32[]{:S(2)}, u32[]{:S(2)}) async-start(f32[32,1,6]{2,1,0:T(1,128)} %bitcast.13), calls=%async_computation.1 | async-start | bytes 32768 | tf_op jit(solution)/shard_map/all_to_all | solution.py:255
  437.4 6.2 %fusion.22 = bf16[1,128,3584]{2,1,0:T(8,128)(2,1)} fusion(bf16[6,256,128]{1,2,0:T(8,128)(2,1)S(1)} %get-tuple-element.25, bf16[6,256,7296]{2,1,0:T(8,128)(2,1)} %shard_map.112, bf16[6,256]{1,0:T(8,128)(2,1)S(1)} %slice_reduce_fusion), kind=kOutput, calls=%fused_computation.15 | convolution fusion | flops 1415249920 | bytes 12323840 | tf_op jit(solution)/shard_map/dot_general | solution.py:251
  443.6 1.1 all-to-all-done.1
  (55 shorter events, 6.9 us)
Async XLA Ops:
  78.8 4.0 copy-start
  78.8 20.6 %copy-start.1 = (bf16[1,3584,128]{2,1,0:T(8,128)(2,1)S(1)}, bf16[1,3584,128]{2,1,0:T(8,128)(2,1)}, u32[]{:S(2)}) copy-start(bf16[1,3584,128]{2,1,0:T(8,128)(2,1)} %param.13) | copy-start | bytes 2752516
  83.3 306.4 %collective-permute-start.2 = (bf16[1,3584,128]{1,2,0:T(8,128)(2,1)S(1)}, bf16[1,3584,128]{1,2,0:T(8,128)(2,1)}, u32[]{:S(2)}, u32[]{:S(2)}) collective-permute-start(bf16[1,3584,128]{1,2,0:T(8,128)(2,1)S(1)} %copy.57), channel_id=1, source_target_pairs={{0,16},{16,0},{1,17},{17,1},{2,18},{18,2},{3,19},{19,3},{4,20},{20... | collective-permute-start | bytes 2752520 | tf_op jit(solution)/shard_map/ppermute | solution.py:21
  99.9 290.1 %collective-permute-start.1 = (bf16[1,3584,128]{1,2,0:T(8,128)(2,1)S(1)}, bf16[1,3584,128]{1,2,0:T(8,128)(2,1)S(1)}, u32[]{:S(2)}, u32[]{:S(2)}) collective-permute-start(bf16[1,3584,128]{1,2,0:T(8,128)(2,1)S(1)} %copy.55), channel_id=1, source_target_pairs={{0,16},{16,0},{1,17},{17,1},{2,18},{18,2},{3,19},{19,3},{4,20},{20... | collective-permute-start | bytes 2752520 | tf_op jit(solution)/shard_map/ppermute | solution.py:21
  100.0 298.6 %collective-permute-start = (bf16[1,128,3584]{2,1,0:T(8,128)(2,1)}, bf16[1,128,3584]{2,1,0:T(8,128)(2,1)}, u32[]{:S(2)}, u32[]{:S(2)}) collective-permute-start(bf16[1,128,3584]{2,1,0:T(8,128)(2,1)} %param.15), channel_id=1, source_target_pairs={{0,16},{16,0},{1,17},{17,1},{2,18},{18,2},{3,19},{19,3},{4,20},{20... | collective-permute-start | bytes 2752520 | tf_op jit(solution)/shard_map/ppermute | solution.py:21
  102.3 286.1 %copy-start.2 = (s32[16]{0:T(128)S(1)}, s32[16]{0:T(128)}, u32[]{:S(2)}) copy-start(s32[16]{0:T(128)} %param.12) | copy-start | bytes 196
  390.0 8.6 %slice-start = ((s8[22413312]{0:T(1024)(128)(4,1)}), s8[4194304]{0:T(1024)(128)(4,1)S(1)}, s32[]{:S(2)}) async-start(s8[22413312]{0:T(1024)(128)(4,1)} %bitcast.38), calls=%async_computation.2 | async-start | bytes 8388608
  390.1 8.5 %slice-start.1 = ((s8[22413312]{0:T(1024)(128)(4,1)}), s8[4194304]{0:T(1024)(128)(4,1)S(1)}, s32[]{:S(2)}) async-start(s8[22413312]{0:T(1024)(128)(4,1)} %bitcast.38), calls=%async_computation.3 | async-start | bytes 8388608
  390.1 8.5 %slice-start.2 = ((s8[22413312]{0:T(1024)(128)(4,1)}), s8[4194304]{0:T(1024)(128)(4,1)S(1)}, s32[]{:S(2)}) async-start(s8[22413312]{0:T(1024)(128)(4,1)} %bitcast.38), calls=%async_computation.4 | async-start | bytes 8388608
  390.1 9.5 %slice-start.3 = ((s8[22413312]{0:T(1024)(128)(4,1)}), s8[4194304]{0:T(1024)(128)(4,1)S(1)}, s32[]{:S(2)}) async-start(s8[22413312]{0:T(1024)(128)(4,1)} %bitcast.38), calls=%async_computation.5 | async-start | bytes 8388608
  390.1 10.6 %slice-start.4 = ((s8[22413312]{0:T(1024)(128)(4,1)}), s8[4194304]{0:T(1024)(128)(4,1)S(1)}, s32[]{:S(2)}) async-start(s8[22413312]{0:T(1024)(128)(4,1)} %bitcast.38), calls=%async_computation.6 | async-start | bytes 8388608
  390.1 11.0 %slice-start.5 = ((s8[22413312]{0:T(1024)(128)(4,1)}), s8[1441792]{0:T(1024)(128)(4,1)S(1)}, s32[]{:S(2)}) async-start(s8[22413312]{0:T(1024)(128)(4,1)} %bitcast.38), calls=%async_computation.7 | async-start | bytes 2883584
  390.1 11.2 %copy-start.3 = (bf16[1,128,3584]{2,1,0:T(8,128)(2,1)S(1)}, bf16[1,128,3584]{2,1,0:T(8,128)(2,1)}, u32[]{:S(2)}) copy-start(bf16[1,128,3584]{2,1,0:T(8,128)(2,1)} %param.15) | copy-start | bytes 2752516
  407.4 12.2 %all-to-all-start = ((f32[8,1,192]{2,1,0:T(1,128)}), f32[8,1,192]{2,1,0:T(1,128)S(1)}, u32[]{:S(2)}, u32[]{:S(2)}) async-start(f32[8,1,192]{2,1,0:T(1,128)} %all_to_all.16), calls=%async_computation | async-start | bytes 16384 | tf_op jit(solution)/shard_map/all_to_all | solution.py:253
  420.4 24.4 %all-to-all-start.1 = ((f32[32,1,6]{2,1,0:T(1,128)}), f32[32,1,6]{2,1,0:T(1,128)S(1)}, u32[]{:S(2)}, u32[]{:S(2)}) async-start(f32[32,1,6]{2,1,0:T(1,128)} %bitcast.13), calls=%async_computation.1 | async-start | bytes 32768 | tf_op jit(solution)/shard_map/all_to_all | solution.py:255
where the time goes:
time: 448 us; the launch traced here: 447 us
  Pallas kernels  346 us (77%)
  starting transfers between devices  39 us (9%)
  matrix products  30.1 us (7%)
  local copies, waits for them, and re-layouts  26.1 us (6%)
    pallas_call x1, Pallas kernels, dp_gather(): pl.pallas_call(functools.partial(dp_gather_kernel, n_dp, ring, chunks), o...  285 us
    pallas_call x1, Pallas kernels, expert_exchange(): pl.pallas_call(functools.partial(expert_exchange_kernel, n_ex), out_shape...  60.9 us
    ppermute x3, starting transfers between devices, partner(): return lax.ppermute(block, axis, route)  18.5 us
    all_to_all x1, starting transfers between devices, body(): lax.all_to_all(own_scores, 'expert', split_axis=0, concat_axis=0, tiled=T...  17 us
    reshape x2, local copies, waits for them, and re-layouts, body(): recv = expert_exchange(packed).reshape(axis_len, CAP, row_width)  10.4 us
  transfers between devices with their start and end apart: 5, of which 2 were waited for; matrix products, arithmetic and copies ran while one was open for 6% of the time, Pallas kernels for 64%

commit v1 on v0

--- a/solution.py
+++ b/solution.py
@@ -70,6 +70,8 @@
         )
     sent.append(push(x_ref, span(me, 0, rows), len(sent), recv.at[me], left))
     sent.append(push(x_ref, span(me, 0, rows), len(sent), recv.at[me], right))
+    local = pltpu.make_async_copy(x_ref, span(me, 0, rows), recv.at[me])
+    local.start()
     arrived(span(left, 0, rows), recv.at[left])
     sent.append(push(span(left, 0, half), span(left, 0, half), len(sent), recv.at[left], right))
     arrived(span(right, 0, rows), recv.at[right])
@@ -89,8 +91,6 @@
     sent.append(
         push(span(right_across, half, half), span(right_across, half, half), len(sent), recv.at[right_across], left)
     )
-    local = pltpu.make_async_copy(x_ref, span(me, 0, rows), recv.at[me])
-    local.start()
     arrived(span(far, 0, rows), recv.at[far])
     far_across = (far + ring) % n_dp
     arrived(span(far_across, 0, rows), recv.at[far_across])

time: 448 us -> 395 us (0.88)
  Pallas kernels: 346 us -> 289 us
    pallas_call x1, Pallas kernels: 285 us -> 228 us  [dp_gather(): pl.pallas_call(functools.partial(dp_gather_kernel, n_dp, ring, chunks), o...]
  transfers between devices with their start and end apart: 5 -> 5, of which waited for: 2 -> 2; matrix products, arithmetic and copies ran while one was open for 6% -> 7% of each run, Pallas kernels for 64% -> 58%
where the time goes in v1:
time: 395 us
  Pallas kernels  289 us (73%)
  starting transfers between devices  41.7 us (11%)
  matrix products  30.4 us (8%)
  local copies, waits for them, and re-layouts  26.1 us (7%)
  other arithmetic  4.19 us (1%)
    pallas_call x1, Pallas kernels, dp_gather(): pl.pallas_call(functools.partial(dp_gather_kernel, n_dp, ring, chunks), o...  228 us
    pallas_call x1, Pallas kernels, expert_exchange(): pl.pallas_call(functools.partial(expert_exchange_kernel, n_ex), out_shape...  60.9 us
    all_to_all x1, starting transfers between devices, body(): lax.all_to_all(own_scores, 'expert', split_axis=0, concat_axis=0, tiled=T...  19.2 us
    ppermute x3, starting transfers between devices, partner(): return lax.ppermute(block, axis, route)  18.5 us
    reshape x2, local copies, waits for them, and re-layouts, body(): recv = expert_exchange(packed).reshape(axis_len, CAP, row_width)  10.4 us
    dot_general x1, matrix products, body(): lax.dot_general(row_x, w_both, feature, preferred_element_type=jnp.float32)  8.46 us
  transfers between devices with their start and end apart: 5, of which 2 were waited for; matrix products, arithmetic and copies ran while one was open for 7% of the time, Pallas kernels for 58%

profile of v1, /device:TPU:1, one launch (start us, length us, event | category | flops | bytes accessed | tf_op | source)
XLA Modules:
  0.0 394.9 jit_solution(228382190531014224)
XLA Ops:
  0.6 0.8 copy.53
  1.5 0.8 copy.48
  2.4 0.7 select_reduce_fusion.1
  4.5 2.3 convolution_convert_fusion
  7.0 4.5 %reshape.127.x_ref = bf16[32,342,128]{2,1,0:T(8,128)(2,1)} reshape(bf16[192,7296]{1,0:T(8,128)(2,1)S(1)} %pad_maximum_fusion) | data formatting | bytes 5603328 | tf_op jit(solution)/shard_map/reshape | solution.py:212
  11.5 60.9 %shard_map.111 = bf16[32,342,128]{2,1,0:T(8,128)(2,1)} custom-call(bf16[32,342,128]{2,1,0:T(8,128)(2,1)} %reshape.127.x_ref), custom_call_target="tpu_custom_call" | custom-call | tf_op jit(solution)/shard_map/pallas_call | solution.py:155
  72.5 6.3 %reshape.128 = bf16[32,6,7296]{2,1,0:T(8,128)(2,1)} reshape(bf16[32,342,128]{2,1,0:T(8,128)(2,1)} %shard_map.111) | data formatting | bytes 5603328 | tf_op jit(solution)/shard_map/reshape | solution.py:213
  78.8 4.0 %copy.68 = bf16[32,6,7296]{2,0,1:T(8,128)(2,1)} copy(bf16[32,6,7296]{2,1,0:T(8,128)(2,1)} %reshape.128) | data formatting | bytes 5603328 | tf_op jit(solution)/shard_map/reshape | solution.py:213
  83.3 16.0 %collective-permute-start.2 = (bf16[1,3584,128]{1,2,0:T(8,128)(2,1)S(1)}, bf16[1,3584,128]{1,2,0:T(8,128)(2,1)}, u32[]{:S(2)}, u32[]{:S(2)}) collective-permute-start(bf16[1,3584,128]{1,2,0:T(8,128)(2,1)S(1)} %copy.57), channel_id=1, source_target_pairs={{0,16},{16,0},{1,17},{17,1},{2,18},{18,2},{3,19},{19,3},{4,20},{20... | collective-permute-start | bytes 2752520 | tf_op jit(solution)/shard_map/ppermute | solution.py:21
  100.0 2.3 collective-permute-start
  102.3 228.4 %shard_map.112 = bf16[6,256,7296]{2,1,0:T(8,128)(2,1)} custom-call(bf16[6,32,7296]{2,1,0:T(8,128)(2,1)} %bitcast.40), custom_call_target="tpu_custom_call" | custom-call | tf_op jit(solution)/shard_map/pallas_call | solution.py:108
  330.7 1.2 slice_reduce_fusion
  333.2 1.4 select_bitcast_fusion
  334.8 8.5 %fusion.7 = f32[6,256,256]{1,2,0:T(8,128)} fusion(bf16[6,256,7296]{2,1,0:T(8,128)(2,1)} %shard_map.112, bf16[3584,128]{0,1:T(8,128)(2,1)S(1)} %select_bitcast_fusion, bf16[3584,128]{0,1:T(8,128)(2,1)S(1)} %select_bitcast_fusion.1), kind=kOutput, calls=%fused_computation.7 | convolution fusion | flops 2822242304 | bytes 14417920 | tf_op jit(solution)/shard_map/dot_general | solution.py:233
  343.3 0.9 slice-done.3
  344.2 1.2 slice-done.4
  346.0 5.5 %multiply_reduce_fusion = (f32[6,256]{1,0:T(8,128)S(1)}, bf16[6,256,128]{1,2,0:T(8,128)(2,1)S(1)}, bf16[6,256,128]{1,2,0:T(8,128)(2,1)S(1)}, bf16[6,256,128]{1,2,0:T(8,128)(2,1)S(1)}) fusion(f32[6,256,256]{1,2,0:T(8,128)} %fusion.7, f32[6,256]{1,0:T(8,128)S(1)} %mul.69, bf16[1,128,3584]{2,1,0:T(8,128)(2,1)} %collective-permute-done, ...), kind=kOutput, calls=%fused_computation.39 | convolution fusion | flops 1413478912 | bytes 15611905 | tf_op jit(solution)/shard_map/dot_general | solution.py:239
  351.6 0.7 all_to_all.16
  352.4 4.0 %all-to-all-start = ((f32[8,1,192]{2,1,0:T(1,128)}), f32[8,1,192]{2,1,0:T(1,128)S(1)}, u32[]{:S(2)}, u32[]{:S(2)}) async-start(f32[8,1,192]{2,1,0:T(1,128)} %all_to_all.16), calls=%async_computation | async-start | bytes 16384 | tf_op jit(solution)/shard_map/all_to_all | solution.py:253
  356.4 7.2 %fusion.13 = bf16[3584,256]{1,0:T(8,128)(2,1)S(1)} fusion(bf16[6,256,7296]{2,1,0:T(8,128)(2,1)} %shard_map.112, bf16[6,256,128]{1,2,0:T(8,128)(2,1)S(1)} %get-tuple-element.31, bf16[6,256,128]{1,2,0:T(8,128)(2,1)S(1)} %get-tuple-element.32), kind=kOutput, calls=%fused_computation.12 | convolution fusion | flops 2821062656 | bytes 13631488 | tf_op jit(solution)/shard_map/dot_general | solution.py:248
  363.6 1.3 slice_bitcast_fusion
  366.1 19.2 %all-to-all-start.1 = ((f32[32,1,6]{2,1,0:T(1,128)}), f32[32,1,6]{2,1,0:T(1,128)S(1)}, u32[]{:S(2)}, u32[]{:S(2)}) async-start(f32[32,1,6]{2,1,0:T(1,128)} %bitcast.13), calls=%async_computation.1 | async-start | bytes 32768 | tf_op jit(solution)/shard_map/all_to_all | solution.py:255
  385.3 6.2 %fusion.22 = bf16[1,128,3584]{2,1,0:T(8,128)(2,1)} fusion(bf16[6,256,128]{1,2,0:T(8,128)(2,1)S(1)} %get-tuple-element.25, bf16[6,256,7296]{2,1,0:T(8,128)(2,1)} %shard_map.112, bf16[6,256]{1,0:T(8,128)(2,1)S(1)} %slice_reduce_fusion), kind=kOutput, calls=%fused_computation.15 | convolution fusion | flops 1415249920 | bytes 12323840 | tf_op jit(solution)/shard_map/dot_general | solution.py:251
  391.5 1.1 all-to-all-done.1
  (55 shorter events, 7.6 us)
Async XLA Ops:
  78.8 4.0 %copy-start = (bf16[1,3584,128]{2,1,0:T(8,128)(2,1)S(1)}, bf16[1,3584,128]{2,1,0:T(8,128)(2,1)}, u32[]{:S(2)}) copy-start(bf16[1,3584,128]{2,1,0:T(8,128)(2,1)} %param.14) | copy-start | bytes 2752516
  78.8 20.6 %copy-start.1 = (bf16[1,3584,128]{2,1,0:T(8,128)(2,1)S(1)}, bf16[1,3584,128]{2,1,0:T(8,128)(2,1)}, u32[]{:S(2)}) copy-start(bf16[1,3584,128]{2,1,0:T(8,128)(2,1)} %param.13) | copy-start | bytes 2752516
  83.3 249.9 %collective-permute-start.2 = (bf16[1,3584,128]{1,2,0:T(8,128)(2,1)S(1)}, bf16[1,3584,128]{1,2,0:T(8,128)(2,1)}, u32[]{:S(2)}, u32[]{:S(2)}) collective-permute-start(bf16[1,3584,128]{1,2,0:T(8,128)(2,1)S(1)} %copy.57), channel_id=1, source_target_pairs={{0,16},{16,0},{1,17},{17,1},{2,18},{18,2},{3,19},{19,3},{4,20},{20... | collective-permute-start | bytes 2752520 | tf_op jit(solution)/shard_map/ppermute | solution.py:21
  99.9 234.7 %collective-permute-start.1 = (bf16[1,3584,128]{1,2,0:T(8,128)(2,1)S(1)}, bf16[1,3584,128]{1,2,0:T(8,128)(2,1)S(1)}, u32[]{:S(2)}, u32[]{:S(2)}) collective-permute-start(bf16[1,3584,128]{1,2,0:T(8,128)(2,1)S(1)} %copy.55), channel_id=1, source_target_pairs={{0,16},{16,0},{1,17},{17,1},{2,18},{18,2},{3,19},{19,3},{4,20},{20... | collective-permute-start | bytes 2752520 | tf_op jit(solution)/shard_map/ppermute | solution.py:21
  100.0 243.3 %collective-permute-start = (bf16[1,128,3584]{2,1,0:T(8,128)(2,1)}, bf16[1,128,3584]{2,1,0:T(8,128)(2,1)}, u32[]{:S(2)}, u32[]{:S(2)}) collective-permute-start(bf16[1,128,3584]{2,1,0:T(8,128)(2,1)} %param.15), channel_id=1, source_target_pairs={{0,16},{16,0},{1,17},{17,1},{2,18},{18,2},{3,19},{19,3},{4,20},{20... | collective-permute-start | bytes 2752520 | tf_op jit(solution)/shard_map/ppermute | solution.py:21
  102.3 229.6 %copy-start.2 = (s32[16]{0:T(128)S(1)}, s32[16]{0:T(128)}, u32[]{:S(2)}) copy-start(s32[16]{0:T(128)} %param.12) | copy-start | bytes 196
  334.6 8.7 %slice-start = ((s8[22413312]{0:T(1024)(128)(4,1)}), s8[4194304]{0:T(1024)(128)(4,1)S(1)}, s32[]{:S(2)}) async-start(s8[22413312]{0:T(1024)(128)(4,1)} %bitcast.38), calls=%async_computation.2 | async-start | bytes 8388608
  334.7 8.5 %slice-start.1 = ((s8[22413312]{0:T(1024)(128)(4,1)}), s8[4194304]{0:T(1024)(128)(4,1)S(1)}, s32[]{:S(2)}) async-start(s8[22413312]{0:T(1024)(128)(4,1)} %bitcast.38), calls=%async_computation.3 | async-start | bytes 8388608
  334.7 8.5 %slice-start.2 = ((s8[22413312]{0:T(1024)(128)(4,1)}), s8[4194304]{0:T(1024)(128)(4,1)S(1)}, s32[]{:S(2)}) async-start(s8[22413312]{0:T(1024)(128)(4,1)} %bitcast.38), calls=%async_computation.4 | async-start | bytes 8388608
  334.7 9.5 %slice-start.3 = ((s8[22413312]{0:T(1024)(128)(4,1)}), s8[4194304]{0:T(1024)(128)(4,1)S(1)}, s32[]{:S(2)}) async-start(s8[22413312]{0:T(1024)(128)(4,1)} %bitcast.38), calls=%async_computation.5 | async-start | bytes 8388608
  334.8 10.6 %slice-start.4 = ((s8[22413312]{0:T(1024)(128)(4,1)}), s8[4194304]{0:T(1024)(128)(4,1)S(1)}, s32[]{:S(2)}) async-start(s8[22413312]{0:T(1024)(128)(4,1)} %bitcast.38), calls=%async_computation.6 | async-start | bytes 8388608
  334.8 11.0 %slice-start.5 = ((s8[22413312]{0:T(1024)(128)(4,1)}), s8[1441792]{0:T(1024)(128)(4,1)S(1)}, s32[]{:S(2)}) async-start(s8[22413312]{0:T(1024)(128)(4,1)} %bitcast.38), calls=%async_computation.7 | async-start | bytes 2883584
  334.8 11.2 %copy-start.3 = (bf16[1,128,3584]{2,1,0:T(8,128)(2,1)S(1)}, bf16[1,128,3584]{2,1,0:T(8,128)(2,1)}, u32[]{:S(2)}) copy-start(bf16[1,128,3584]{2,1,0:T(8,128)(2,1)} %param.15) | copy-start | bytes 2752516
  352.4 13.0 %all-to-all-start = ((f32[8,1,192]{2,1,0:T(1,128)}), f32[8,1,192]{2,1,0:T(1,128)S(1)}, u32[]{:S(2)}, u32[]{:S(2)}) async-start(f32[8,1,192]{2,1,0:T(1,128)} %all_to_all.16), calls=%async_computation | async-start | bytes 16384 | tf_op jit(solution)/shard_map/all_to_all | solution.py:253
  366.1 26.6 %all-to-all-start.1 = ((f32[32,1,6]{2,1,0:T(1,128)}), f32[32,1,6]{2,1,0:T(1,128)S(1)}, u32[]{:S(2)}, u32[]{:S(2)}) async-start(f32[32,1,6]{2,1,0:T(1,128)} %bitcast.13), calls=%async_computation.1 | async-start | bytes 32768 | tf_op jit(solution)/shard_map/all_to_all | solution.py:255

commit v2 on v1

--- a/solution.py
+++ b/solution.py
@@ -21,7 +21,7 @@
     return lax.ppermute(block, axis, route)
 
 
-def dp_gather_kernel(n_dp, ring, chunks, x_ref, o_ref, recv, recv_z, send):
+def dp_gather_kernel(n_dp, ring, chunks, x_ref, o_ref, recv, recv_z, send, stage, stage_sem):
     me = lax.axis_index("dp")
     ex = lax.axis_index("expert")
     rows = x_ref.shape[1]
@@ -70,7 +70,10 @@
         )
     sent.append(push(x_ref, span(me, 0, rows), len(sent), recv.at[me], left))
     sent.append(push(x_ref, span(me, 0, rows), len(sent), recv.at[me], right))
-    local = pltpu.make_async_copy(x_ref, span(me, 0, rows), recv.at[me])
+    staged = pltpu.make_async_copy(x_ref, stage, stage_sem.at[0])
+    staged.start()
+    staged.wait()
+    local = pltpu.make_async_copy(stage, span(me, 0, rows), recv.at[me])
     local.start()
     arrived(span(left, 0, rows), recv.at[left])
     sent.append(push(span(left, 0, half), span(left, 0, half), len(sent), recv.at[left], right))
@@ -114,8 +117,12 @@
             pltpu.SemaphoreType.DMA((n_dp,)),
             pltpu.SemaphoreType.DMA((chunks,)),
             pltpu.SemaphoreType.DMA((sends,)),
+            pltpu.VMEM(block.shape, block.dtype),
+            pltpu.SemaphoreType.DMA((1,)),
         ],
-        compiler_params=pltpu.CompilerParams(collective_id=0, has_side_effects=True),
+        compiler_params=pltpu.CompilerParams(
+            collective_id=0, has_side_effects=True, vmem_limit_bytes=32 * 1024 * 1024
+        ),
     )(block)
 
 

time: 395 us -> 396 us (level)
  transfers between devices with their start and end apart: 5 -> 5, of which waited for: 2 -> 2; matrix products, arithmetic and copies ran while one was open for 7% -> 7% of each run, Pallas kernels for 58% -> 57%
where the time goes in v2:
time: 396 us
  Pallas kernels  288 us (73%)
  starting transfers between devices  42.4 us (11%)
  matrix products  30.2 us (8%)
  local copies, waits for them, and re-layouts  27.9 us (7%)
  other arithmetic  4.12 us (1%)
    pallas_call x1, Pallas kernels, dp_gather(): pl.pallas_call(functools.partial(dp_gather_kernel, n_dp, ring, chunks), o...  227 us
    pallas_call x1, Pallas kernels, expert_exchange(): pl.pallas_call(functools.partial(expert_exchange_kernel, n_ex), out_shape...  60.9 us
    all_to_all x1, starting transfers between devices, body(): lax.all_to_all(own_scores, 'expert', split_axis=0, concat_axis=0, tiled=T...  20 us
    ppermute x3, starting transfers between devices, partner(): return lax.ppermute(block, axis, route)  18.3 us
    reshape x2, local copies, waits for them, and re-layouts, body(): recv = expert_exchange(packed).reshape(axis_len, CAP, row_width)  8.67 us
    dot_general x1, matrix products, body(): lax.dot_general(row_x, w_both, feature, preferred_element_type=jnp.float32)  8.46 us
  transfers between devices with their start and end apart: 5, of which 2 were waited for; matrix products, arithmetic and copies ran while one was open for 7% of the time, Pallas kernels for 57%

profile of v2, /device:TPU:1, one launch (start us, length us, event | category | flops | bytes accessed | tf_op | source)
XLA Modules:
  0.0 395.6 jit_solution(5431412686921820346)
XLA Ops:
  0.6 0.8 copy.53
  1.5 0.8 copy.48
  4.5 2.3 convolution_convert_fusion
  7.0 4.5 %reshape.127.x_ref = bf16[32,342,128]{2,1,0:T(8,128)(2,1)} reshape(bf16[192,7296]{1,0:T(8,128)(2,1)S(1)} %pad_maximum_fusion) | data formatting | bytes 5603328 | tf_op jit(solution)/shard_map/reshape | solution.py:219
  11.5 60.9 %shard_map.111 = bf16[32,342,128]{2,1,0:T(8,128)(2,1)} custom-call(bf16[32,342,128]{2,1,0:T(8,128)(2,1)} %reshape.127.x_ref), custom_call_target="tpu_custom_call" | custom-call | tf_op jit(solution)/shard_map/pallas_call | solution.py:162
  72.5 6.3 %reshape.128 = bf16[32,6,7296]{2,1,0:T(8,128)(2,1)} reshape(bf16[32,342,128]{2,1,0:T(8,128)(2,1)} %shard_map.111) | data formatting | bytes 5603328 | tf_op jit(solution)/shard_map/reshape | solution.py:220
  78.8 2.3 copy.68
  81.1 2.2 copy.57
  83.4 15.9 %collective-permute-start.2 = (bf16[1,3584,128]{1,2,0:T(8,128)(2,1)}, bf16[1,3584,128]{1,2,0:T(8,128)(2,1)}, u32[]{:S(2)}, u32[]{:S(2)}) collective-permute-start(bf16[1,3584,128]{1,2,0:T(8,128)(2,1)} %copy.57), channel_id=1, source_target_pairs={{0,16},{16,0},{1,17},{17,1},{2,18},{18,2},{3,19},{19,3},{4,20},{20... | collective-permute-start | bytes 2752520 | tf_op jit(solution)/shard_map/ppermute | solution.py:21
  99.3 2.2 copy.55
  101.5 2.4 collective-permute-start
  103.9 227.0 %shard_map.112 = bf16[6,256,7296]{2,1,0:T(8,128)(2,1)} custom-call(bf16[6,32,7296]{2,1,0:T(8,128)(2,1)S(1)} %bitcast.38), custom_call_target="tpu_custom_call" | custom-call | tf_op jit(solution)/shard_map/pallas_call | solution.py:111
  330.9 1.3 slice_reduce_fusion
  333.5 1.3 select_bitcast_fusion
  335.0 8.5 %fusion.7 = f32[6,256,256]{1,2,0:T(8,128)} fusion(bf16[6,256,7296]{2,1,0:T(8,128)(2,1)} %shard_map.112, bf16[3584,128]{0,1:T(8,128)(2,1)S(1)} %select_bitcast_fusion, bf16[3584,128]{0,1:T(8,128)(2,1)S(1)} %select_bitcast_fusion.1), kind=kOutput, calls=%fused_computation.7 | convolution fusion | flops 2822242304 | bytes 14417920 | tf_op jit(solution)/shard_map/dot_general | solution.py:240
  343.4 0.9 slice-done.3
  344.4 1.2 slice-done.4
  346.1 5.3 %multiply_reduce_fusion = (f32[6,256]{1,0:T(8,128)S(1)}, bf16[6,256,128]{1,2,0:T(8,128)(2,1)S(1)}, bf16[6,256,128]{1,2,0:T(8,128)(2,1)S(1)}, bf16[6,256,128]{1,2,0:T(8,128)(2,1)S(1)}) fusion(f32[6,256,256]{1,2,0:T(8,128)} %fusion.7, f32[6,256]{1,0:T(8,128)S(1)} %mul.69, bf16[1,128,3584]{2,1,0:T(8,128)(2,1)} %collective-permute-done, ...), kind=kOutput, calls=%fused_computation.39 | convolution fusion | flops 1413478912 | bytes 15611905 | tf_op jit(solution)/shard_map/dot_general | solution.py:246
  352.3 4.1 %all-to-all-start = ((f32[8,1,192]{2,1,0:T(1,128)}), f32[8,1,192]{2,1,0:T(1,128)S(1)}, u32[]{:S(2)}, u32[]{:S(2)}) async-start(f32[8,1,192]{2,1,0:T(1,128)} %all_to_all.16), calls=%async_computation | async-start | bytes 16384 | tf_op jit(solution)/shard_map/all_to_all | solution.py:260
  356.3 7.2 %fusion.13 = bf16[3584,256]{1,0:T(8,128)(2,1)S(1)} fusion(bf16[6,256,7296]{2,1,0:T(8,128)(2,1)} %shard_map.112, bf16[6,256,128]{1,2,0:T(8,128)(2,1)S(1)} %get-tuple-element.31, bf16[6,256,128]{1,2,0:T(8,128)(2,1)S(1)} %get-tuple-element.32), kind=kOutput, calls=%fused_computation.12 | convolution fusion | flops 2821062656 | bytes 13631488 | tf_op jit(solution)/shard_map/dot_general | solution.py:255
  363.5 1.3 slice_bitcast_fusion
  366.0 20.0 %all-to-all-start.1 = ((f32[32,1,6]{2,1,0:T(1,128)}), f32[32,1,6]{2,1,0:T(1,128)S(1)}, u32[]{:S(2)}, u32[]{:S(2)}) async-start(f32[32,1,6]{2,1,0:T(1,128)} %bitcast.13), calls=%async_computation.1 | async-start | bytes 32768 | tf_op jit(solution)/shard_map/all_to_all | solution.py:262
  386.0 6.2 %fusion.22 = bf16[1,128,3584]{2,1,0:T(8,128)(2,1)} fusion(bf16[6,256,128]{1,2,0:T(8,128)(2,1)S(1)} %get-tuple-element.25, bf16[6,256,7296]{2,1,0:T(8,128)(2,1)} %shard_map.112, bf16[6,256]{1,0:T(8,128)(2,1)S(1)} %slice_reduce_fusion), kind=kOutput, calls=%fused_computation.15 | convolution fusion | flops 1415249920 | bytes 12323840 | tf_op jit(solution)/shard_map/dot_general | solution.py:258
  392.2 1.1 all-to-all-done.1
  (53 shorter events, 8.0 us)
Async XLA Ops:
  83.4 250.1 %collective-permute-start.2 = (bf16[1,3584,128]{1,2,0:T(8,128)(2,1)}, bf16[1,3584,128]{1,2,0:T(8,128)(2,1)}, u32[]{:S(2)}, u32[]{:S(2)}) collective-permute-start(bf16[1,3584,128]{1,2,0:T(8,128)(2,1)} %copy.57), channel_id=1, source_target_pairs={{0,16},{16,0},{1,17},{17,1},{2,18},{18,2},{3,19},{19,3},{4,20},{20... | collective-permute-start | bytes 2752520 | tf_op jit(solution)/shard_map/ppermute | solution.py:21
  101.5 233.2 %collective-permute-start.1 = (bf16[1,3584,128]{1,2,0:T(8,128)(2,1)}, bf16[1,3584,128]{1,2,0:T(8,128)(2,1)}, u32[]{:S(2)}, u32[]{:S(2)}) collective-permute-start(bf16[1,3584,128]{1,2,0:T(8,128)(2,1)} %copy.55), channel_id=1, source_target_pairs={{0,16},{16,0},{1,17},{17,1},{2,18},{18,2},{3,19},{19,3},{4,20},{20... | collective-permute-start | bytes 2752520 | tf_op jit(solution)/shard_map/ppermute | solution.py:21
  101.5 241.9 %collective-permute-start = (bf16[1,128,3584]{2,1,0:T(8,128)(2,1)}, bf16[1,128,3584]{2,1,0:T(8,128)(2,1)}, u32[]{:S(2)}, u32[]{:S(2)}) collective-permute-start(bf16[1,128,3584]{2,1,0:T(8,128)(2,1)} %param.15), channel_id=1, source_target_pairs={{0,16},{16,0},{1,17},{17,1},{2,18},{18,2},{3,19},{19,3},{4,20},{20... | collective-permute-start | bytes 2752520 | tf_op jit(solution)/shard_map/ppermute | solution.py:21
  103.9 228.3 %copy-start.1 = (s32[16]{0:T(128)S(1)}, s32[16]{0:T(128)}, u32[]{:S(2)}) copy-start(s32[16]{0:T(128)} %param.12) | copy-start | bytes 196
  330.9 3.9 copy-start
  334.8 8.7 %slice-start = ((s8[22413312]{0:T(1024)(128)(4,1)}), s8[4194304]{0:T(1024)(128)(4,1)S(1)}, s32[]{:S(2)}) async-start(s8[22413312]{0:T(1024)(128)(4,1)} %bitcast.39), calls=%async_computation.2 | async-start | bytes 8388608
  334.9 8.5 %slice-start.1 = ((s8[22413312]{0:T(1024)(128)(4,1)}), s8[4194304]{0:T(1024)(128)(4,1)S(1)}, s32[]{:S(2)}) async-start(s8[22413312]{0:T(1024)(128)(4,1)} %bitcast.39), calls=%async_computation.3 | async-start | bytes 8388608
  334.9 8.5 %slice-start.2 = ((s8[22413312]{0:T(1024)(128)(4,1)}), s8[4194304]{0:T(1024)(128)(4,1)S(1)}, s32[]{:S(2)}) async-start(s8[22413312]{0:T(1024)(128)(4,1)} %bitcast.39), calls=%async_computation.4 | async-start | bytes 8388608
  334.9 9.4 %slice-start.3 = ((s8[22413312]{0:T(1024)(128)(4,1)}), s8[4194304]{0:T(1024)(128)(4,1)S(1)}, s32[]{:S(2)}) async-start(s8[22413312]{0:T(1024)(128)(4,1)} %bitcast.39), calls=%async_computation.5 | async-start | bytes 8388608
  334.9 10.6 %slice-start.4 = ((s8[22413312]{0:T(1024)(128)(4,1)}), s8[4194304]{0:T(1024)(128)(4,1)S(1)}, s32[]{:S(2)}) async-start(s8[22413312]{0:T(1024)(128)(4,1)} %bitcast.39), calls=%async_computation.6 | async-start | bytes 8388608
  334.9 11.0 %slice-start.5 = ((s8[22413312]{0:T(1024)(128)(4,1)}), s8[1441792]{0:T(1024)(128)(4,1)S(1)}, s32[]{:S(2)}) async-start(s8[22413312]{0:T(1024)(128)(4,1)} %bitcast.39), calls=%async_computation.7 | async-start | bytes 2883584
  334.9 11.2 %copy-start.2 = (bf16[1,128,3584]{2,1,0:T(8,128)(2,1)S(1)}, bf16[1,128,3584]{2,1,0:T(8,128)(2,1)}, u32[]{:S(2)}) copy-start(bf16[1,128,3584]{2,1,0:T(8,128)(2,1)} %param.15) | copy-start | bytes 2752516
  352.3 13.0 %all-to-all-start = ((f32[8,1,192]{2,1,0:T(1,128)}), f32[8,1,192]{2,1,0:T(1,128)S(1)}, u32[]{:S(2)}, u32[]{:S(2)}) async-start(f32[8,1,192]{2,1,0:T(1,128)} %all_to_all.16), calls=%async_computation | async-start | bytes 16384 | tf_op jit(solution)/shard_map/all_to_all | solution.py:260
  366.0 27.3 %all-to-all-start.1 = ((f32[32,1,6]{2,1,0:T(1,128)}), f32[32,1,6]{2,1,0:T(1,128)S(1)}, u32[]{:S(2)}, u32[]{:S(2)}) async-start(f32[32,1,6]{2,1,0:T(1,128)} %bitcast.13), calls=%async_computation.1 | async-start | bytes 32768 | tf_op jit(solution)/shard_map/all_to_all | solution.py:262
